TPU v7x, 32 devices: a whole 2x2x4 slice. The times are simulated.
32 devices in a mesh: rows: 8 (over z, y), cols: 4 (over x, core).
Axes of the slice: x: 2, y: 2, z: 4, core: 2. Of those that a mesh axis runs over, the one named last changes fastest.
Arguments:
- coefficients: float32 [4, 1024, 4, 256], P(None, 'rows'), may hold values from -0.03 to 0.09
- support: int32 [4, 1024, 4], P(None, 'rows'), may hold values from 0 to 11, all different within a row
- primal: float32 [12, 256, 256], P('cols'), may hold values from -0.5 to 9, as said below
- dual_inverse: float32 [12, 256, 256], P('cols'), may hold values from -0.5 to 9, as said below
- block_sizes: int32 [12], P('cols'), may hold values from 64 to 256, as said below
- damping: float32 [4, 1024], P(None, 'rows'), may hold values from 0.5 to 2
- right_sides: float32 [4, 32, 1024], P(None, 'cols', 'rows'), may hold values from -6 to 6
Outputs:
- updated: float32 [4, 1024, 4096], P(None, 'rows', 'cols')
- panel_factor: float32 [4, 1024, 128], P(None, 'rows')
- solved: float32 [4, 32, 1024], P(None, 'cols', 'rows')
Inputs may be any that keep to these rules, and one draw needn't show every extreme that they name: `primal`: each block is symmetric positive definite. `dual_inverse`: each block is symmetric positive definite. `block_sizes`: some block has order 256.
All inputs are finite; a program needn't handle non-finite values.
Results may differ from a plain program's by a relative error of at most 0.00015.
Values sent between devices are 32-bit elements; how exact they have to be, the bound alone decides.
A program may use at most 192 MiB of HBM per device.

v0:
```python
import functools

import jax
import jax.numpy as jnp
from jax import lax
from jax.experimental import pallas as pl
from jax.experimental.pallas import tpu as pltpu
from jax.sharding import PartitionSpec as P

TILE = 128

MESH = pl.DeviceIdType.MESH
highest = lax.Precision.HIGHEST


def split(x):
    top = x.astype(jnp.bfloat16)
    return top, (x - top.astype(jnp.float32)).astype(jnp.bfloat16)


def product(a, b, dims):
    return lax.dot_general(a, b, (dims, ((), ())), preferred_element_type=jnp.float32)


def three(a_top, a_low, b_top, b_low, dims):
    return product(a_top, b_top, dims) + (product(a_top, b_low, dims) + product(a_low, b_top, dims))


def select_block(coef, label, b):
    pieces = []
    for h in range(0, 2):
        acc = None
        for k in range(coef.slots):
            hit = label(k) == b
            value = coef(k, h)
            acc = jnp.where(hit, value, jnp.zeros_like(value) if acc is None else acc)
        pieces.append(acc)
    return jnp.concatenate(pieces, axis=1)


class Rows:
    def __init__(self, read, slots):
        self.read, self.slots = read, slots

    def __call__(self, k, h):
        return self.read(k, pl.ds(h * TILE, TILE))


def exchange(rows, cols, small_ref, w_ref, own_ref, own_names_ref,
             schur_out, lead_schur_out, inverse_out, small_out,
             tiles_out, names_out, leads_out, w_out, label_own, label_col, lead_sc, d_top, d_low, c_top, c_low,
             g_top, g_low, acc, work,
             local_sem, fwd_s, fwd_r, bwd_s, bwd_r, name_s, name_r, lead_s, lead_r, share_s, share_r, small_s, small_r,
             wx_s, wx_r, wp_s, wp_r):
    r = lax.axis_index("rows")
    c = lax.axis_index("cols")
    half = rows // 2
    odd = r % 2
    pos = (1 - odd) * (r // 2) + odd * (rows - 1 - r // 2)

    def row_at(p):
        p = (p + rows) % rows
        upper = p // half
        return (1 - upper) * (2 * p) + upper * (2 * (rows - 1 - p) + 1)

    right = row_at(pos + 1)
    left = row_at(pos - 1)
    partner = c + 1 - 2 * (c % 2)

    def send(src, dst, s, v, row=None, col=None):
        return pltpu.make_async_remote_copy(
            src_ref=src, dst_ref=dst, send_sem=s, recv_sem=v,
            device_id=(r if row is None else row, c if col is None else col), device_id_type=MESH)

    barrier = pltpu.get_barrier_semaphore()
    for d in range(1, rows):
        pl.semaphore_signal(barrier, inc=1, device_id=((r + d) % rows, c), device_id_type=MESH)
    for d in range(1, cols):
        pl.semaphore_signal(barrier, inc=1, device_id=(r, (c + d) % cols), device_id_type=MESH)
    pl.semaphore_wait(barrier, rows + cols - 2)

    own_blocks = w_ref.shape[0]
    blocks = w_out.shape[0]
    height = own_ref.shape[1]
    slots = own_ref.shape[0]
    layer = (c * (height * rows // cols)) // (rows * TILE)
    tile_ref = own_ref.at[:, pl.ds(pl.multiple_of(layer * TILE, TILE), TILE)]
    names_ref = own_names_ref.at[layer]
    chunk = TILE // cols
    lead_ref = own_ref.at[:, pl.ds(pl.multiple_of(c * chunk, chunk), chunk)]
    cut = slots // 2
    part = (pl.ds(0, cut), pl.ds(cut, slots - cut))

    own = [pltpu.make_async_copy(tile_ref, tiles_out.at[r], local_sem.at[0]),
           pltpu.make_async_copy(names_ref, names_out.at[r], local_sem.at[1])]
    for copy in own:
        copy.start()

    waits = []
    def weight(source, i):
        return w_out.at[source * own_blocks + i]

    for i in range(own_blocks):
        copy = send(w_ref.at[i], weight(c, i), wp_s.at[0, i], wp_r.at[0, i], col=partner)
        copy.start()
        waits.append(copy)
        for k in range(1, cols // 2):
            copy = send(w_ref.at[i], weight(c, i), wx_s.at[k, i], wx_r.at[k, i], col=(c + 2 * k) % cols)
            copy.start()
            waits.append(copy)

    for d in range(1, rows):
        copy = send(names_ref, names_out.at[r], name_s.at[d], name_r.at[d], row=(r + d) % rows)
        copy.start()
        waits.append(copy)

    lead_row = [send(lead_ref, leads_out.at[c], lead_s.at[0], lead_r.at[0], row=right),
                send(lead_ref, leads_out.at[c], lead_s.at[1], lead_r.at[0], row=left)]

    @pl.when(r == 0)
    def _():
        for copy in lead_row:
            copy.start()
        for d in range(1, rows):
            send(small_ref, small_out, small_s.at[d], small_r.at[0], row=d).start()
        pltpu.make_async_copy(lead_ref, leads_out.at[c], local_sem.at[3]).start()
        pltpu.make_async_copy(small_ref, small_out, local_sem.at[4]).start()

    def first(h):
        send(tile_ref.at[part[h]], tiles_out.at[r, part[h]], fwd_s.at[0, h], fwd_r.at[0, h], row=right).start()
        send(tile_ref.at[part[h]], tiles_out.at[r, part[h]], bwd_s.at[0, h], bwd_r.at[0, h], row=left).start()

    first(0)
    near = jnp.minimum(pos, rows - pos)

    @pl.when(near >= 2)
    def _():
        first(1)

    def put_labels(dst, at, names):
        turned = jnp.transpose(names)
        for k in range(slots):
            dst[k, pl.ds(at, TILE), :] = jnp.broadcast_to(turned[:, k:k + 1], (TILE, TILE))

    for t in range(height // TILE):
        put_labels(label_own, t * TILE, own_names_ref[t])
    full = height // TILE

    def arrived(k, i):
        send(w_ref.at[i], weight(c, i), wp_s.at[k, i], wp_r.at[k, i], col=partner).wait_recv()

    def forward(i):
        if i < own_blocks:
            for k in range(1, cols // 2):
                send(w_ref.at[i], weight(c, i), wx_s.at[k, i], wx_r.at[k, i], col=(c + 2 * k) % cols).wait_recv()
                source = (c + cols - 2 * k) % cols
                copy = send(weight(source, i), weight(source, i), wp_s.at[k, i], wp_r.at[k, i], col=partner)
                copy.start()
                waits.append(copy)

    def weigh(source, held, tiles_high):
        first_tile, stop = tiles_high
        span = pl.ds(first_tile * TILE, (stop - first_tile) * TILE)
        for i in range(own_blocks):
            b = source * own_blocks + i
            name = b.astype(jnp.float32)
            side = i % 2
            for t in range(first_tile, stop):
                at = pl.ds(t * TILE, TILE)
                if t < full:
                    coef = Rows(lambda k, lanes: own_ref[k, at, lanes], slots)
                else:
                    coef = Rows(lambda k, lanes: lead_sc[k, :, lanes], slots)
                top, low = split(select_block(coef, lambda k: label_own[k, at, :], name))
                d_top[side, at, :] = top
                d_low[side, at, :] = low
            w_top, w_low = split(w_out[b] if held is None else held[i])
            top, low = split(three(d_top[side, span, :], d_low[side, span, :], w_top, w_low, ((1,), (0,))))
            g_top[b, span, :] = top
            g_low[b, span, :] = low

    weigh(c, w_ref, tiles_high=(0, full))

    relay_right = send(leads_out.at[c], leads_out.at[c], lead_s.at[0], lead_r.at[0], row=right)
    relay_left = send(leads_out.at[c], leads_out.at[c], lead_s.at[1], lead_r.at[0], row=left)

    @pl.when(r != 0)
    def _():
        relay_right.wait_recv()

    @pl.when((pos >= 1) & (pos < half))
    def _():
        relay_right.start()

    @pl.when(pos >= half + 2)
    def _():
        relay_left.start()

    @pl.when(r == 0)
    def _():
        pltpu.make_async_copy(lead_ref, leads_out.at[c], local_sem.at[3]).wait()
        pltpu.make_async_copy(small_ref, small_out, local_sem.at[4]).wait()

    for d in range(1, cols):
        copy = send(leads_out.at[c], leads_out.at[c], share_s.at[d], share_r.at[d], col=(c + d) % cols)
        copy.start()
        waits.append(copy)

    @pl.when(near < 2)
    def _():
        first(1)

    last = half - 1

    def ring(s, h):
        ahead = row_at(pos - s)
        behind = row_at(pos + s)
        send(tile_ref.at[part[h]], tiles_out.at[r, part[h]], fwd_s.at[s - 1, h], fwd_r.at[s - 1, h], row=right).wait_recv()
        if s < last or h == 0:
            send(tiles_out.at[ahead, part[h]], tiles_out.at[ahead, part[h]], fwd_s.at[s, h], fwd_r.at[s, h], row=right).start()
        send(tile_ref.at[part[h]], tiles_out.at[r, part[h]], bwd_s.at[s - 1, h], bwd_r.at[s - 1, h], row=left).wait_recv()
        if s < last or h == 1:
            send(tiles_out.at[behind, part[h]], tiles_out.at[behind, part[h]], bwd_s.at[s, h], bwd_r.at[s, h], row=left).start()

    for i in range(own_blocks):
        arrived(0, i)
    weigh(partner, None, tiles_high=(0, full))
    pending = [(s, h) for s in range(1, half) for h in range(2)]

    def serve(count):
        for _ in range(count):
            if pending:
                ring(*pending.pop(0))

    serve(2)
    forward(0)
    for d in range(1, cols):
        send(leads_out.at[c], leads_out.at[c], share_s.at[d], share_r.at[d], col=(c + d) % cols).wait_recv()

    @pl.when(r != 0)
    def _():
        send(small_ref, small_out, small_s.at[0], small_r.at[0], row=0).wait_recv()

    for d in range(1, rows):
        send(names_ref, names_out.at[r], name_s.at[d], name_r.at[d], row=(r + d) % rows).wait_recv()
    for copy in own:
        copy.wait()
    for q in range(cols):
        lead_sc[:, q * chunk:(q + 1) * chunk, :] = leads_out[q]
    put_labels(label_own, height, small_out[0:8, :])
    forward(1)
    weigh(c, w_ref, tiles_high=(full, full + 1))
    weigh(partner, None, tiles_high=(full, full + 1))
    serve(1)
    for i in range(2, own_blocks):
        forward(i)
    for k in range(1, cols // 2):
        weigh((c + cols - 2 * k) % cols, None, tiles_high=(0, full + 1))
        serve(1)
    for k in range(1, cols // 2):
        for i in range(own_blocks):
            arrived(k, i)
        weigh((partner + cols - 2 * k) % cols, None, tiles_high=(0, full + 1))

    lane = lax.broadcasted_iota(jnp.int32, (TILE, TILE), 1)
    line = lax.broadcasted_iota(jnp.int32, (TILE, TILE), 0)

    def eliminate(j):
        at = jnp.minimum(j, TILE - 1)
        pivot = work[pl.ds(at, 1), :]
        column = jnp.sum(jnp.where(lane == at, work[:, :TILE], 0.0), axis=1, keepdims=True)
        scale = jnp.sum(jnp.where(lane[0:1] == at, pivot[:, :TILE], 0.0), axis=1, keepdims=True)
        factor = jnp.where(line[:, 0:1] > j, column, 0.0) / scale
        work[...] = work[...] - factor * pivot

    fold = max(u for u in range(1, 5) if blocks % u == 0)
    rounds = blocks // fold
    steps = -(-TILE // ((half - 1) * rounds))

    def group(tiles, step=None):
        width = len(tiles) * TILE
        for i, row in enumerate(tiles):
            put_labels(label_col, i * TILE, small_out[0:8, :] if row is None else names_out[row])
        acc[:, :width] = jnp.zeros((acc.shape[0], width), jnp.float32)

        def body(n, carry):
            for u in range(fold):
                name = (n * fold + u).astype(jnp.float32)
                for i, row in enumerate(tiles):
                    at = pl.ds(i * TILE, TILE)
                    if row is None:
                        coef = Rows(lambda k, lanes: lead_sc[k, :, lanes], slots)
                    else:
                        coef = Rows(lambda k, lanes: tiles_out[row, k, :, lanes], slots)
                    top, low = split(select_block(coef, lambda k: label_col[k, at, :], name))
                    c_top[u, at, :] = top
                    c_low[u, at, :] = low
            a_top = [g_top[n * fold + u] for u in range(fold)]
            a_low = [g_low[n * fold + u] for u in range(fold)]
            b_top = [c_top[u, :width, :] for u in range(fold)]
            b_low = [c_low[u, :width, :] for u in range(fold)]
            acc[:, :width] += product(
                jnp.concatenate(a_top + a_top + a_low, axis=1), jnp.concatenate(b_top + b_low + b_top, axis=1), ((1,), (1,)))
            if step is not None:
                for e in range(steps):
                    eliminate(step + n * steps + e)
            return carry

        lax.fori_loop(0, rounds, body, 0)
        for i, row in enumerate(tiles):
            value = acc[:, i * TILE:(i + 1) * TILE]
            if row is None:
                lead_schur_out[...] = value
            else:
                schur_out[:, pl.ds(pl.multiple_of(row * TILE, TILE), TILE)] = value

    group([None, r])
    serve(1)

    work[:, :TILE] = lead_schur_out[height:, :] + jnp.where(lane == line, jnp.broadcast_to(small_out[7:8, :], (TILE, TILE)), 0.0)
    work[:, TILE:] = jnp.where(lane == line, 1.0, 0.0)

    for g in range(1, half):
        while pending and pending[0][0] <= g:
            serve(1)
        group([row_at(pos - g), row_at(pos + g)], (g - 1) * rounds * steps)
        serve(1)
    send(tile_ref.at[part[0]], tiles_out.at[r, part[0]], fwd_s.at[last, 0], fwd_r.at[last, 0], row=right).wait_recv()
    send(tile_ref.at[part[1]], tiles_out.at[r, part[1]], bwd_s.at[last, 1], bwd_r.at[last, 1], row=left).wait_recv()
    diagonal = jnp.sum(jnp.where(lane == line, work[:, :TILE], 0.0), axis=1, keepdims=True)
    inverse_out[...] = work[:, TILE:] / jnp.sqrt(diagonal)
    group([row_at(pos + half)])

    for s in range(half):
        for h in range(2):
            if s < last or h == 0:
                send(tile_ref.at[part[h]], tiles_out.at[r, part[h]], fwd_s.at[s, h], fwd_r.at[s, h], row=right).wait_send()
            if s < last or h == 1:
                send(tile_ref.at[part[h]], tiles_out.at[r, part[h]], bwd_s.at[s, h], bwd_r.at[s, h], row=left).wait_send()

    for copy in waits:
        copy.wait_send()
    @pl.when(r == 0)
    def _():
        for copy in lead_row:
            copy.wait_send()
        for d in range(1, rows):
            send(small_ref, small_out, small_s.at[d], small_r.at[0], row=d).wait_send()

    @pl.when((pos >= 1) & (pos < half))
    def _():
        relay_right.wait_send()

    @pl.when(pos >= half + 2)
    def _():
        relay_left.wait_send()


def assemble(rows, cols, small, weights, own, own_names):
    half = rows // 2
    dma = pltpu.SemaphoreType.DMA
    vmem = pl.BlockSpec(memory_space=pltpu.VMEM)
    slots, height, order = own.shape
    blocks = cols * weights.shape[0]
    tall = height + TILE
    f32, bf16 = jnp.float32, jnp.bfloat16
    return pl.pallas_call(
        functools.partial(exchange, rows, cols),
        out_shape=[
            jax.ShapeDtypeStruct((tall, rows * TILE), f32),
            jax.ShapeDtypeStruct((tall, TILE), f32),
            jax.ShapeDtypeStruct((TILE, TILE), f32),
            jax.ShapeDtypeStruct(small.shape, f32),
        ],
        in_specs=[vmem] * 4,
        out_specs=[vmem] * 4,
        scratch_shapes=[
            pltpu.VMEM((rows, slots, TILE, order), f32),
            pltpu.VMEM((rows,) + own_names.shape[1:], f32),
            pltpu.VMEM((cols, slots, TILE // cols, order), f32),
            pltpu.VMEM((blocks, order, order), f32),
            pltpu.VMEM((slots, tall, TILE), f32),
            pltpu.VMEM((slots, 2 * TILE, TILE), f32),
            pltpu.VMEM((slots, TILE, order), f32),
            pltpu.VMEM((2, tall, order), bf16),
            pltpu.VMEM((2, tall, order), bf16),
            pltpu.VMEM((4, 2 * TILE, order), bf16),
            pltpu.VMEM((4, 2 * TILE, order), bf16),
            pltpu.VMEM((blocks, tall, order), bf16),
            pltpu.VMEM((blocks, tall, order), bf16),
            pltpu.VMEM((tall, 2 * TILE), f32),
            pltpu.VMEM((TILE, 2 * TILE), f32),
        ]
        + [dma((5,))] + [dma((half, 2))] * 4 + [dma((rows,))] * 2 + [dma((2,)), dma((1,))]
        + [dma((cols,))] * 2 + [dma((rows,)), dma((1,))] + [dma((cols, weights.shape[0]))] * 4,
        compiler_params=pltpu.CompilerParams(collective_id=0, has_side_effects=True),
    )(small, weights, own, own_names)


def local(coefficients, support, primal, dual_inverse, block_sizes, damping, right_sides):
    col_index = lax.axis_index("cols")
    row_index = lax.axis_index("rows")
    rows = lax.axis_size("rows")
    cols = lax.axis_size("cols")
    layers, _, slots, order = coefficients.shape
    span = TILE * rows
    count_all = layers * span
    col_width = count_all // cols
    sides = right_sides.shape[1]
    positions = jnp.arange(order, dtype=jnp.int32)
    active = (positions[None, :] < block_sizes[:, None]).astype(jnp.float32)
    weights = primal * dual_inverse * active[:, :, None] * active[:, None, :]

    own_names = jnp.pad(jnp.transpose(support, (0, 2, 1)).astype(jnp.float32), ((0, 0), (0, 8 - slots), (0, 0)))
    small = jnp.concatenate([
        own_names[0][:7],
        damping[0][None, :],
        jnp.pad(right_sides[0], ((0, -sides % 8), (0, 0)))], axis=0)
    own = jnp.transpose(coefficients, (2, 0, 1, 3)).reshape(slots, layers * TILE, order)
    schur_rows, own_lead, inverse, small = assemble(rows, cols, small, weights, own, own_names)
    if span != col_width:
        schur_rows = lax.dynamic_slice_in_dim(schur_rows, (col_index * col_width) % span, col_width, 1)
    lead_damping = small[7]
    top_sides = small[8:8 + sides]

    row_global = ((jnp.arange(layers)[:, None] * rows + row_index) * TILE + jnp.arange(TILE)[None, :]).reshape(-1)
    col_global = col_index * col_width + jnp.arange(col_width)
    flat_damping = damping.reshape(-1)
    schur = schur_rows[:layers * TILE] + jnp.where(row_global[:, None] == col_global[None, :], flat_damping[:, None], 0.0)
    lead_ids = jnp.arange(TILE)
    panel_raw = own_lead[:layers * TILE] + jnp.where(row_global[:, None] == lead_ids[None, :], flat_damping[:, None], 0.0)
    column_raw = schur_rows[layers * TILE:] + jnp.where(lead_ids[:, None] == col_global[None, :], lead_damping[:, None], 0.0)
    panel_factor = jnp.einsum("ak,jk->aj", panel_raw, inverse, precision=highest)
    column_panel = jnp.einsum("jk,kn->jn", inverse, column_raw, precision=highest)
    outer_term = jnp.dot(panel_factor, column_panel, precision=highest)
    row_later = row_global >= TILE
    col_later = col_global >= TILE
    updated = schur - jnp.where(row_later[:, None] & col_later[None, :], outer_term, 0.0)
    leading = jnp.einsum("sk,jk->sj", top_sides, inverse, precision=highest)
    panel_factor = panel_factor.reshape(layers, TILE, TILE)
    remainder = right_sides - jnp.einsum("sk,tak->tsa", leading, panel_factor, precision=highest)
    solved = jnp.where(row_later.reshape(layers, TILE)[:, None, :], remainder, leading[None, :, :])
    return (updated.reshape(layers, TILE, col_width), panel_factor, solved)


def solution(mesh):
    in_specs = (
        P(None, "rows", None, None),
        P(None, "rows", None),
        P("cols", None, None),
        P("cols", None, None),
        P("cols"),
        P(None, "rows"),
        P(None, "cols", "rows"),
    )
    out_specs = (P(None, "rows", "cols"), P(None, "rows", None), P(None, "cols", "rows"))
    return jax.shard_map(local, mesh=mesh, in_specs=in_specs, out_specs=out_specs, check_vma=False)
```

profile of v0, /device:TPU:22, one launch (start us, length us, event | category | flops | bytes accessed | tf_op | source)
XLA Modules:
  0.0 86.1 jit_solution(1125252558017889981)
XLA Ops:
  0.6 0.7 convert_bitcast_fusion
  1.3 0.7 slice_bitcast_fusion
  2.0 0.7 slice.31
  2.7 0.6 pad_maximum_fusion.small_ref
  3.3 0.6 pad.4.own_names_ref
  3.9 0.0 copy-start.7
  3.9 0.0 copy-start.1
  3.9 0.0 copy-start.2
  3.9 3.4 %copy.10 = f32[4,4,128,256]{3,2,1,0:T(8,128)} copy(f32[4,4,128,256]{3,0,2,1:T(4,128)} %bitcast.35) | data formatting | bytes 4194304 | tf_op jit(solution)/shard_map/transpose | solution.py:419
  7.4 0.0 copy-done.7
  7.4 0.1 fusion.19
  7.4 0.0 copy-done.1
  7.4 0.0 copy-done.2
  7.4 1.1 %multiply_multiply_fusion.w_ref = f32[3,256,256]{2,1,0:T(8,128)} fusion(f32[3,256,256]{2,1,0:T(8,128)S(1)} %copy-done.1, f32[3,256,256]{2,1,0:T(8,128)S(1)} %copy-done.2, f32[3,256]{1,0:T(4,128)S(1)} %fusion.19), kind=kLoop, calls=%fused_computation.4 | loop fusion | flops 589824 | bytes 2362368 | tf_op jit(solution)/shard_map/mul | solution.py:412
  8.5 67.1 %shard_map.94 = (f32[640,1024]{1,0:T(8,128)}, f32[640,128]{1,0:T(8,128)}, f32[128,128]{1,0:T(8,128)}, f32[16,128]{1,0:T(8,128)}) custom-call(f32[16,128]{1,0:T(8,128)} %pad_maximum_fusion.small_ref, f32[3,256,256]{2,1,0:T(8,128)} %multiply_multiply_fusion.w_ref, f32[4,512,256]{2,1,0:T(8,128)} %bitcast.32, f32[4,8,128]{2,1,0:T(8,128)} %pad.4.own_names_ref), custom_call_target="tpu_custom_call" | custom-call | tf_op jit(solution)/shard_map/pallas_call | solution.py:367
  75.6 0.7 slice_bitcast_fusion.2
  76.3 1.8 %fusion.2 = f32[128,1024]{1,0:T(8,128)S(1)} fusion(f32[128,128]{1,0:T(8,128)} %get-tuple-element.9, f32[640,1024]{1,0:T(8,128)} %get-tuple-element.7, f32[128]{0:T(128)S(1)} %slice_bitcast_fusion.2, s32[1024]{0:T(1024)S(1)} %iota_add_fusion), kind=kOutput, calls=%fused_computation.5 | convolution fusion | flops 201719808 | bytes 1118720 | tf_op jit(solution)/shard_map/jk,kn->jn/dot_general | solution.py:434
  78.1 0.1 fusion.21
  78.2 0.0 copy-done.5
  78.2 1.4 %fusion.9 = f32[512,128]{1,0:T(8,128)S(1)} fusion(f32[128,128]{1,0:T(8,128)} %get-tuple-element.9, f32[640,128]{1,0:T(8,128)} %get-tuple-element.8, f32[512]{0:T(512)S(1)} %bitcast.37, s32[512]{0:T(512)S(1)} %fusion.21), kind=kOutput, calls=%fused_computation.13 | convolution fusion | flops 100859904 | bytes 593920 | tf_op jit(solution)/shard_map/ak,jk->aj/dot_general | solution.py:433
  79.6 0.0 copy-start
  79.6 0.1 broadcast_compare_fusion.1
  79.7 0.0 copy-start.6
  79.7 0.0 copy-start.4
  79.7 5.1 %select_subtract_fusion = f32[512,1024]{1,0:T(8,128)} fusion(f32[640,1024]{1,0:T(8,128)} %get-tuple-element.7, f32[512,128]{1,0:T(8,128)S(1)} %fusion.9, f32[128,1024]{1,0:T(8,128)S(1)} %fusion.2, f32[512]{0:T(512)S(1)} %bitcast.38, s32[1024]{0:T(1024)S(1)} %iota_add_fusion, s32[512]{0:T(512)S(1)} %fusion.21, pred[1024]{0:T(1024)(128)(4,1)S(1)} %broadcast_compare_fusion, ...), kind=kOutput, calls=%fused_computation | convolution fusion | flops 808452096 | bytes 4990464 | tf_op jit(solution)/shard_map/dot_general | solution.py:435
  84.8 0.0 copy-done.3
  84.8 0.0 copy-done.6
  84.8 0.2 fusion.17
  85.0 0.1 fusion.20
  85.1 0.0 copy-done
  85.1 0.0 copy-done.4
  85.1 1.0 %fusion.1 = f32[4,8,128]{2,1,0:T(8,128)} fusion(f32[4,8,128]{2,1,0:T(8,128)S(1)} %copy-done.4, f32[4,128,128]{2,1,0:T(8,128)S(1)} %bitcast.33, f32[8,128]{1,0:T(8,128)S(1)} %fusion.17, pred[4,128]{1,0:T(4,128)(4,1)S(1)} %fusion.20), kind=kOutput, calls=%fused_computation.3 | convolution fusion | flops 6299648 | bytes 299520 | tf_op jit(solution)/shard_map/sk,tak->tsa/dot_general | solution.py:441
  (6 shorter events, 0.0 us)
Async XLA Ops:
  3.9 3.4 %copy-start.7 = (s32[3]{0:T(128)S(1)}, s32[3]{0:T(128)}, u32[]{:S(2)}) copy-start(s32[3]{0:T(128)} %param.11) | copy-start | bytes 40
  3.9 3.5 %copy-start.1 = (f32[3,256,256]{2,1,0:T(8,128)S(1)}, f32[3,256,256]{2,1,0:T(8,128)}, u32[]{:S(2)}) copy-start(f32[3,256,256]{2,1,0:T(8,128)} %param.9) | copy-start | bytes 2359300
  3.9 3.5 %copy-start.2 = (f32[3,256,256]{2,1,0:T(8,128)S(1)}, f32[3,256,256]{2,1,0:T(8,128)}, u32[]{:S(2)}) copy-start(f32[3,256,256]{2,1,0:T(8,128)} %param.10) | copy-start | bytes 2359300
  8.5 69.6 %copy-start.5 = (f32[4,128]{1,0:T(4,128)S(1)}, f32[4,128]{1,0:T(4,128)}, u32[]{:S(2)}) copy-start(f32[4,128]{1,0:T(4,128)} %param.12) | copy-start | bytes 6148
  79.6 5.5 %copy-start = (f32[512,128]{1,0:T(8,128)}, f32[512,128]{1,0:T(8,128)S(1)}, u32[]{:S(2)}) copy-start(f32[512,128]{1,0:T(8,128)S(1)} %fusion.9) | copy-start | bytes 786436
  79.7 5.2 %copy-start.3 = (f32[128,128]{1,0:T(8,128)S(1)}, f32[128,128]{1,0:T(8,128)}, u32[]{:S(2)}) copy-start(f32[128,128]{1,0:T(8,128)} %get-tuple-element.9) | copy-start | bytes 196612
  79.7 5.2 %copy-start.6 = (f32[16,128]{1,0:T(8,128)S(1)}, f32[16,128]{1,0:T(8,128)}, u32[]{:S(2)}) copy-start(f32[16,128]{1,0:T(8,128)} %get-tuple-element.10) | copy-start | bytes 24580
  79.7 5.4 %copy-start.4 = (f32[4,8,128]{2,1,0:T(8,128)S(1)}, f32[4,8,128]{2,1,0:T(8,128)}, u32[]{:S(2)}) copy-start(f32[4,8,128]{2,1,0:T(8,128)} %param.13) | copy-start | bytes 49156
where the time goes:
time: 86.5 us; the launch traced here: 86.1 us
  Pallas kernels  67.1 us (78%)
  matrix products  9.49 us (11%)
  local copies, waits for them, and re-layouts  6.13 us (7%)
  other arithmetic  2.69 us (3%)
    pallas_call x1, Pallas kernels, assemble(): pl.pallas_call(functools.partial(exchange, rows, cols), out_shape=[jax.Sh...  67.1 us
    dot_general x1, matrix products, local(): outer_term = jnp.dot(panel_factor, column_panel, precision=highest)  5.13 us
    transpose x1, local copies, waits for them, and re-layouts, local(): jnp.transpose(coefficients, (2, 0, 1, 3))  3.43 us
    dot_general x1, matrix products, local(): jnp.einsum('jk,kn->jn', inverse, column_raw, precision=highest)  1.78 us

commit v1 on v0

v1 whole, which is shorter than its diff:
```python
import functools

import jax
import jax.numpy as jnp
from jax import lax
from jax.experimental import pallas as pl
from jax.experimental.pallas import tpu as pltpu
from jax.sharding import PartitionSpec as P

TILE = 128

MESH = pl.DeviceIdType.MESH
highest = lax.Precision.HIGHEST
f32, bf16 = jnp.float32, jnp.bfloat16


def split(x):
    top = x.astype(bf16)
    return top, (x - top.astype(f32)).astype(bf16)


def product(a, b, dims, precision=None):
    return lax.dot_general(a, b, (dims, ((), ())), precision=precision, preferred_element_type=f32)


def exchange(rows, cols, coef_ref, primal_ref, dual_ref, sizes_ref, names_ref, damp_ref, sides_ref,
             updated_out, panel_out, solved_out,
             tiles, names_all, own, leads, lead_names, lead_damp, lead_sides, primal, dual, w_all,
             own_hi, own_lo, label_own, col_hi, col_lo, label_col, d_top, d_low, c_top, c_low,
             g_top, g_low, acc, schur, lead_schur, work, q_cat,
             local_sem, out_sem, fwd_s, fwd_r, bwd_s, bwd_r, fname_s, fname_r, bname_s, bname_r,
             lead_s, lead_r, share_s, share_r, pass_s, pass_r, wx_s, wx_r, wp_s, wp_r):
    r = lax.axis_index("rows")
    c = lax.axis_index("cols")
    half = rows // 2
    last = half - 1
    odd = r % 2
    pos = (1 - odd) * (r // 2) + odd * (rows - 1 - r // 2)

    def row_at(p):
        p = (p + rows) % rows
        upper = p // half
        return (1 - upper) * (2 * p) + upper * (2 * (rows - 1 - p) + 1)

    right = row_at(pos + 1)
    left = row_at(pos - 1)
    partner = c + 1 - 2 * (c % 2)
    near = jnp.minimum(pos, rows - pos)
    far = range(1, cols // 2)

    layers, lines, _ = coef_ref.shape
    slots = names_ref.shape[1]
    own_blocks, order, _ = primal_ref.shape
    blocks = cols * own_blocks
    height = layers * TILE
    full = layers
    groups = order // TILE
    layer = (c * (height * rows // cols)) // (rows * TILE)
    chunk = lines // cols

    def send(src, dst, s, v, row=None, col=None):
        return pltpu.make_async_remote_copy(
            src_ref=src, dst_ref=dst, send_sem=s, recv_sem=v,
            device_id=(r if row is None else row, c if col is None else col), device_id_type=MESH)

    loads = [pltpu.make_async_copy(primal_ref, primal, local_sem.at[0]),
             pltpu.make_async_copy(dual_ref, dual, local_sem.at[1]),
             pltpu.make_async_copy(coef_ref, own, local_sem.at[2])]
    for copy in loads:
        copy.start()

    barrier = pltpu.get_barrier_semaphore()
    for row in (right, left):
        pl.semaphore_signal(barrier, inc=1, device_id=(row, c), device_id_type=MESH)
    pl.semaphore_signal(barrier, inc=1, device_id=(r, partner), device_id_type=MESH)
    for k in far:
        pl.semaphore_signal(barrier, inc=1, device_id=(r, (c + 2 * k) % cols), device_id_type=MESH)

    loads[0].wait()
    loads[1].wait()
    across = lax.broadcasted_iota(jnp.int32, (order, order), 1)
    along = lax.broadcasted_iota(jnp.int32, (order, order), 0)
    for i in range(own_blocks):
        size = sizes_ref[i]
        w_all[c * own_blocks + i] = jnp.where((along < size) & (across < size), primal[i] * dual[i], 0.0)
    pl.semaphore_wait(barrier, 3 + len(far))

    waits = []

    def part(h):
        return pl.ds(h * (lines // 2), lines // 2)

    def fwd(s, h):
        row = row_at(pos - s)
        src = coef_ref.at[layer, part(h)] if s == 0 else tiles.at[row, part(h)]
        return send(src, tiles.at[row, part(h)], fwd_s.at[s, h], fwd_r.at[s, h], row=right)

    def bwd(s, h):
        row = row_at(pos + s)
        src = coef_ref.at[layer, part(h)] if s == 0 else tiles.at[row, part(h)]
        return send(src, tiles.at[row, part(h)], bwd_s.at[s, h], bwd_r.at[s, h], row=left)

    def fwd_name(s):
        row = row_at(pos - s)
        src = names_ref.at[layer] if s == 0 else names_all.at[row]
        return send(src, names_all.at[row], fname_s.at[s], fname_r.at[s], row=right)

    def bwd_name(s):
        row = row_at(pos + s)
        src = names_ref.at[layer] if s == 0 else names_all.at[row]
        return send(src, names_all.at[row], bname_s.at[s], bname_r.at[s], row=left)

    mine = pl.ds(pl.multiple_of(c * chunk, chunk), chunk)
    lead_own = [(coef_ref.at[0, mine], leads.at[mine]), (names_ref.at[0], lead_names),
                (damp_ref, lead_damp), (sides_ref.at[0], lead_sides)]
    lead_all = [(leads.at[mine], leads.at[mine]), (lead_names, lead_names),
                (lead_damp, lead_damp), (lead_sides, lead_sides)]

    def lead_to(pieces, way, row):
        return [send(src, dst, lead_s.at[way, m], lead_r.at[m], row=row) for m, (src, dst) in enumerate(pieces)]

    lead_local = [pltpu.make_async_copy(src, dst, local_sem.at[3 + m]) for m, (src, dst) in enumerate(lead_own)]

    @pl.when(r == 0)
    def _():
        for copy in lead_to(lead_own, 0, right) + lead_to(lead_own, 1, left) + lead_local:
            copy.start()

    def first(h):
        fwd(0, h).start()
        bwd(0, h).start()

    def wx(k, i, source=None):
        b = (c if source is None else source) * own_blocks + i
        return send(w_all.at[b], w_all.at[b], wx_s.at[k, i], wx_r.at[k, i], col=(c + 2 * k) % cols)

    def wp(k, i, source):
        b = source * own_blocks + i
        return send(w_all.at[b], w_all.at[b], wp_s.at[k, i], wp_r.at[k, i], col=partner)

    first(0)
    fwd_name(0).start()
    bwd_name(0).start()
    for i in range(own_blocks):
        for k in far:
            wx(k, i).start()
            waits.append(wx(k, i))
        wp(0, i, c).start()
        waits.append(wp(0, i, c))

    @pl.when(near >= 2)
    def _():
        first(1)

    def unpack(raw, hi, lo, at):
        for k in range(slots):
            for h in range(groups):
                top, low = split(raw[pl.ds(h * slots + k, TILE, stride=slots * groups), :])
                hi[k, at, h * TILE:(h + 1) * TILE] = top
                lo[k, at, h * TILE:(h + 1) * TILE] = low

    def put_labels(dst, at, names):
        names = names.astype(f32)
        turned = jnp.transpose(jnp.concatenate([names] * (8 // slots), axis=0))
        for k in range(slots):
            dst[k, at, :] = jnp.broadcast_to(turned[:, k:k + 1], (TILE, TILE)).astype(bf16)

    def called(b):
        return jnp.full((TILE, TILE), b.astype(f32)).astype(bf16)

    def pick(source, name):
        hi, lo, label, at = source
        top = low = jnp.zeros((TILE, order), bf16)
        for k in range(slots):
            hit = label[k, at, :] == name
            hit = jnp.concatenate([hit] * groups, axis=1)
            top = jnp.where(hit, hi[k, at, :], top)
            low = jnp.where(hit, lo[k, at, :], low)
        return top, low

    def own_tile(t):
        at = t * TILE
        return own_hi, own_lo, label_own, pl.ds(at if isinstance(t, int) else pl.multiple_of(at, TILE), TILE)

    def weigh(b, begin, stop):
        name = called(b)
        for t in range(begin, stop):
            top, low = pick(own_tile(t), name)
            at = pl.ds(t * TILE, TILE)
            d_top[at, :] = top
            d_low[at, :] = low
        span = pl.ds(begin * TILE, (stop - begin) * TILE)
        w_top, w_low = split(w_all[b])
        top, low = split(product(
            jnp.concatenate([d_top[span, :], d_top[span, :], d_low[span, :]], axis=1),
            jnp.concatenate([w_top, w_low, w_top], axis=0), ((1,), (0,))))
        g_top[b, span, :] = top
        g_low[b, span, :] = low

    loads[2].wait()
    for t in range(full):
        put_labels(label_own, pl.ds(t * TILE, TILE), names_ref[t])
        unpack(own.at[t], own_hi, own_lo, pl.ds(t * TILE, TILE))

    def weigh_source(source):
        def body(i, carry):
            weigh(source * own_blocks + i, 0, full)
            return carry
        lax.fori_loop(0, own_blocks, body, 0)

    weigh_source(c)

    def lead_step():
        @pl.when(r != 0)
        def _():
            for copy in lead_to(lead_all, 0, right):
                copy.wait_recv()

        @pl.when((pos >= 1) & (pos < half))
        def _():
            for copy in lead_to(lead_all, 0, right):
                copy.start()

        @pl.when(pos >= half + 2)
        def _():
            for copy in lead_to(lead_all, 1, left):
                copy.start()

        @pl.when(r == 0)
        def _():
            for copy in lead_local:
                copy.wait()

        for k in far:
            share(k).start()
        hand(0, c).start()

    def share(k):
        return send(leads.at[mine], leads.at[mine], share_s.at[k], share_r.at[k], col=(c + 2 * k) % cols)

    def piece(source):
        return pl.ds(pl.multiple_of(source * chunk, chunk), chunk)

    def hand(k, source):
        return send(leads.at[piece(source)], leads.at[piece(source)], pass_s.at[k], pass_r.at[k], col=partner)

    def ring(s, h):
        fwd(s - 1, h).wait_recv()
        if s < last or h == 0:
            fwd(s, h).start()
        bwd(s - 1, h).wait_recv()
        if s < last or h == 1:
            bwd(s, h).start()
        if h == 0:
            fwd_name(s - 1).wait_recv()
            bwd_name(s - 1).wait_recv()
            fwd_name(s).start()
            if s < last:
                bwd_name(s).start()

    def forward(i):
        for k in far:
            source = (c + cols - 2 * k) % cols
            wx(k, i).wait_recv()
            wp(k, i, source).start()
            waits.append(wp(k, i, source))

    def weigh_far(i):
        def body(j, carry):
            k = 1 + j // 2
            side = j % 2
            source = ((1 - side) * c + side * partner + cols - 2 * k) % cols
            weigh(source * own_blocks + i, 0, full)
            return carry
        for k in far:
            wp(k, i, c).wait_recv()
        lax.fori_loop(0, 2 * len(far), body, 0)

    pl.when(near < 3)(lead_step)

    @pl.when(near < 2)
    def _():
        first(1)

    for i in range(own_blocks):
        wp(0, i, c).wait_recv()
    weigh_source(partner)
    pending = [(s, h) for s in range(1, half) for h in range(2)]

    def serve(count):
        for _ in range(count):
            if pending:
                ring(*pending.pop(0))

    serve(1)
    forward(0)
    if own_blocks > 1:
        forward(1)
    pl.when(near == 3)(lead_step)
    serve(1)
    for i in range(2, own_blocks):
        forward(i)
    for i in range(min(2, own_blocks)):
        weigh_far(i)
    serve(1)
    pl.when(near > 3)(lead_step)
    for i in range(2, own_blocks):
        weigh_far(i)
    for k in far:
        share(k).wait_recv()
        hand(k, (c + cols - 2 * k) % cols).start()
    hand(0, c).wait_recv()
    for k in far:
        hand(k, c).wait_recv()

    put_labels(label_own, pl.ds(height, TILE), lead_names[...])
    unpack(leads, own_hi, own_lo, pl.ds(height, TILE))

    def weigh_lead(b, carry):
        weigh(b, full, full + 1)
        return carry

    lax.fori_loop(0, blocks, weigh_lead, 0)

    lane = lax.broadcasted_iota(jnp.int32, (TILE, TILE), 1)
    line = lax.broadcasted_iota(jnp.int32, (TILE, TILE), 0)
    fold = max(u for u in range(1, 5) if blocks % u == 0)
    rounds = blocks // fold
    low_rows = pl.ds(height, TILE)

    def double(sources, begin, size):
        acc[:2 * size, :] = jnp.zeros((2 * size, 2 * TILE), f32)

        def body(n, carry):
            for u in range(fold):
                top, low = pick(sources, called(n * fold + u))
                c_top[u, :TILE, :] = top
                c_top[u, TILE:, :] = low
            span = pl.ds(begin, size)
            a_top = jnp.concatenate([g_top[n * fold + u, span, :] for u in range(fold)], axis=1)
            a_low = jnp.concatenate([g_low[n * fold + u, span, :] for u in range(fold)], axis=1)
            both = jnp.concatenate([c_top[u] for u in range(fold)], axis=1)
            acc[:2 * size, :] += product(jnp.concatenate([a_top, a_low], axis=0), both, ((1,), (1,)))
            return carry

        lax.fori_loop(0, rounds, body, 0)
        return (acc[:size, :TILE] + (acc[:size, TILE:] + acc[size:2 * size, :TILE])) + acc[size:2 * size, TILE:]

    def eye(values):
        return jnp.where(lane == line, jnp.broadcast_to(values, (TILE, TILE)), 0.0)

    work[:, :TILE] = double(own_tile(full), height, TILE) + eye(lead_damp[0:1, :])
    work[:, TILE:] = jnp.where(lane == line, 1.0, 0.0)

    def eliminate(j):
        at = jnp.minimum(j, TILE - 1)
        pivot = work[pl.ds(at, 1), :]
        column = jnp.sum(jnp.where(lane == at, work[:, :TILE], 0.0), axis=1, keepdims=True)
        scale = jnp.sum(jnp.where(lane[0:1] == at, pivot[:, :TILE], 0.0), axis=1, keepdims=True)
        factor = jnp.where(line[:, 0:1] > j, column, 0.0) / scale
        work[...] = work[...] - factor * pivot

    steps = -(-TILE // (half * rounds))
    tall = height + TILE

    def group(sources, outs, begin):
        acc[:tall, :] = jnp.zeros((tall, 2 * TILE), f32)

        def body(n, carry):
            for u in range(fold):
                name = called(n * fold + u)
                for i, source in enumerate(sources):
                    at = pl.ds(i * TILE, TILE)
                    top, low = pick(source, name)
                    c_top[u, at, :] = top
                    c_low[u, at, :] = low
            a_top = [g_top[n * fold + u] for u in range(fold)]
            a_low = [g_low[n * fold + u] for u in range(fold)]
            b_top = [c_top[u] for u in range(fold)]
            b_low = [c_low[u] for u in range(fold)]
            acc[:tall, :] += product(
                jnp.concatenate(a_top + a_top + a_low, axis=1), jnp.concatenate(b_top + b_low + b_top, axis=1), ((1,), (1,)))
            for e in range(steps):
                eliminate(begin + n * steps + e)
            return carry

        lax.fori_loop(0, rounds, body, 0)
        for i, out in enumerate(outs):
            if out is None:
                lead_schur[...] = acc[:tall, i * TILE:(i + 1) * TILE]
            else:
                schur[:, columns(out)] = acc[:tall, i * TILE:(i + 1) * TILE]

    def columns(row):
        return pl.ds(pl.multiple_of(row * TILE, TILE), TILE)

    def remote(row, i):
        at = pl.ds(i * TILE, TILE)
        unpack(tiles.at[row], col_hi, col_lo, at)
        put_labels(label_col, at, names_all[row])
        return col_hi, col_lo, label_col, at

    group([own_tile(full), own_tile(layer)], [None, r], 0)
    here = pl.ds(pl.multiple_of(layer * TILE, TILE), TILE)
    schur[here, columns(r)] = schur[here, columns(r)] + eye(damp_ref[pl.ds(layer, 1), :])
    serve(1)
    for g in range(1, half):
        while pending and pending[0][0] <= g:
            serve(1)
        ahead, behind = row_at(pos - g), row_at(pos + g)
        group([remote(ahead, 0), remote(behind, 1)], [ahead, behind], g * rounds * steps)
        serve(1)

    diagonal = jnp.sum(jnp.where(lane == line, work[:, :TILE], 0.0), axis=1, keepdims=True)
    inverse = work[:, TILE:] / jnp.sqrt(diagonal)
    top_row = (r == 0).astype(f32)
    lead_schur[:TILE, :] = lead_schur[:TILE, :] + eye(damp_ref[0:1, :]) * top_row
    panel = product(lead_schur[:height, :], inverse, ((1,), (1,)), highest)
    panel_out[...] = panel
    q = product(panel, inverse, ((1,), (0,)), highest)
    q = jnp.concatenate([q[:TILE] * (1.0 - top_row), q[TILE:]], axis=0)
    q_top, q_low = split(q)
    q_cat[...] = jnp.concatenate([q_top, q_top, q_low], axis=1)
    leading = product(lead_sides[...], inverse, ((1,), (1,)), highest)
    remainder = product(leading, panel, ((1,), (1,)), highest)
    for t in range(layers):
        value = sides_ref[t] - remainder[:, t * TILE:(t + 1) * TILE]
        solved_out[t] = jnp.where(r == 0, leading, value) if t == 0 else value

    def leave(row, slot):
        return pltpu.make_async_copy(
            schur.at[pl.ds(0, height), columns(row)], updated_out.at[:, columns(row)], out_sem.at[slot])

    def finish(d, carry):
        row = row_at(pos + half + d)
        keep = 1.0 - ((layer + row) == 0).astype(f32)
        s_top, s_low = split(schur[low_rows, columns(row)] * keep)
        schur[pl.ds(0, height), columns(row)] = schur[pl.ds(0, height), columns(row)] - product(
            q_cat[...], jnp.concatenate([s_top, s_low, s_top], axis=0), ((1,), (0,)))
        leave(row, d).start()
        return carry

    lax.fori_loop(1, rows, finish, 0)

    fwd(last, 0).wait_recv()
    fwd_name(last).wait_recv()
    bwd(last, 1).wait_recv()
    opposite = row_at(pos + half)
    schur[:, columns(opposite)] = double(remote(opposite, 0), 0, tall)
    finish(0, 0)

    for s in range(half):
        for h in range(2):
            if s < last or h == 0:
                fwd(s, h).wait_send()
            if s < last or h == 1:
                bwd(s, h).wait_send()
        fwd_name(s).wait_send()
        if s < last:
            bwd_name(s).wait_send()
    for copy in waits:
        copy.wait_send()
    for k in far:
        share(k).wait_send()
        hand(k, (c + cols - 2 * k) % cols).wait_send()
    hand(0, c).wait_send()

    @pl.when(r == 0)
    def _():
        for copy in lead_to(lead_own, 0, right) + lead_to(lead_own, 1, left):
            copy.wait_send()

    @pl.when((pos >= 1) & (pos < half))
    def _():
        for copy in lead_to(lead_all, 0, right):
            copy.wait_send()

    @pl.when(pos >= half + 2)
    def _():
        for copy in lead_to(lead_all, 1, left):
            copy.wait_send()

    def leaving(d, carry):
        leave(row_at(pos + half + d), d).wait()
        return carry

    lax.fori_loop(0, rows, leaving, 0)


def assemble(rows, cols, coef, primal, dual, sizes, names, damping, sides):
    half = rows // 2
    dma = pltpu.SemaphoreType.DMA
    vmem = pl.BlockSpec(memory_space=pltpu.VMEM)
    anywhere = pl.BlockSpec(memory_space=pl.ANY)
    layers, lines, _ = coef.shape
    slots = names.shape[1]
    own_blocks, order, _ = primal.shape
    blocks = cols * own_blocks
    height = layers * TILE
    tall = height + TILE
    return pl.pallas_call(
        functools.partial(exchange, rows, cols),
        out_shape=[
            jax.ShapeDtypeStruct((height, rows * TILE), f32),
            jax.ShapeDtypeStruct((height, TILE), f32),
            jax.ShapeDtypeStruct(sides.shape, f32),
        ],
        in_specs=[anywhere] * 3 + [pl.BlockSpec(memory_space=pltpu.SMEM)] + [vmem] * 3,
        out_specs=[anywhere, vmem, vmem],
        scratch_shapes=[
            pltpu.VMEM((rows, lines, TILE), f32),
            pltpu.VMEM((rows,) + names.shape[1:], jnp.int32),
            pltpu.VMEM(coef.shape, f32),
            pltpu.VMEM((lines, TILE), f32),
            pltpu.VMEM(names.shape[1:], jnp.int32),
            pltpu.VMEM(damping.shape, f32),
            pltpu.VMEM(sides.shape[1:], f32),
            pltpu.VMEM(primal.shape, f32),
            pltpu.VMEM(dual.shape, f32),
            pltpu.VMEM((blocks, order, order), f32),
            pltpu.VMEM((slots, tall, order), bf16),
            pltpu.VMEM((slots, tall, order), bf16),
            pltpu.VMEM((slots, tall, TILE), bf16),
            pltpu.VMEM((slots, 2 * TILE, order), bf16),
            pltpu.VMEM((slots, 2 * TILE, order), bf16),
            pltpu.VMEM((slots, 2 * TILE, TILE), bf16),
            pltpu.VMEM((tall, order), bf16),
            pltpu.VMEM((tall, order), bf16),
            pltpu.VMEM((4, 2 * TILE, order), bf16),
            pltpu.VMEM((4, 2 * TILE, order), bf16),
            pltpu.VMEM((blocks, tall, order), bf16),
            pltpu.VMEM((blocks, tall, order), bf16),
            pltpu.VMEM((2 * tall, 2 * TILE), f32),
            pltpu.VMEM((tall, rows * TILE), f32),
            pltpu.VMEM((tall, TILE), f32),
            pltpu.VMEM((TILE, 2 * TILE), f32),
            pltpu.VMEM((height, 3 * TILE), bf16),
        ]
        + [dma((7,)), dma((rows,))] + [dma((half, 2))] * 4 + [dma((half,))] * 4 + [dma((2, 4)), dma((4,))]
        + [dma((cols,))] * 4 + [dma((cols, own_blocks))] * 4,
        compiler_params=pltpu.CompilerParams(collective_id=0, has_side_effects=True),
    )(coef, primal, dual, sizes, names, damping, sides)


def local(coefficients, support, primal, dual_inverse, block_sizes, damping, right_sides):
    col_index = lax.axis_index("cols")
    rows = lax.axis_size("rows")
    cols = lax.axis_size("cols")
    layers, tile, slots, order = coefficients.shape
    groups = order // TILE
    span = TILE * rows
    col_width = layers * span // cols
    coef = coefficients.reshape(layers, tile, slots, groups, TILE).transpose(0, 1, 3, 2, 4)
    coef = coef.reshape(layers, tile * slots * groups, TILE)
    names = jnp.transpose(support, (0, 2, 1))
    updated, panel, solved = assemble(rows, cols, coef, primal, dual_inverse, block_sizes, names, damping, right_sides)
    if span != col_width:
        updated = lax.dynamic_slice_in_dim(updated, (col_index * col_width) % span, col_width, 1)
    return updated.reshape(layers, tile, col_width), panel.reshape(layers, tile, TILE), solved


def solution(mesh):
    in_specs = (
        P(None, "rows", None, None),
        P(None, "rows", None),
        P("cols", None, None),
        P("cols", None, None),
        P("cols"),
        P(None, "rows"),
        P(None, "cols", "rows"),
    )
    out_specs = (P(None, "rows", "cols"), P(None, "rows", None), P(None, "cols", "rows"))
    return jax.shard_map(local, mesh=mesh, in_specs=in_specs, out_specs=out_specs, check_vma=False)
```

time: 86.5 us -> 70.7 us (0.82)
  the two profiles are of different devices: /device:TPU:22 before, /device:TPU:29 now
where the time goes in v1:
time: 70.7 us; the launch traced here: 70.5 us
  Pallas kernels  65.3 us (92%)
  local copies, waits for them, and re-layouts  4.52 us (6%)
    pallas_call x1, Pallas kernels, assemble(): pl.pallas_call(functools.partial(exchange, rows, cols), out_shape=[jax.Sh...  65.3 us
    unnamed x7, local copies, waits for them, and re-layouts  4.52 us

profile of v1, /device:TPU:29, one launch (start us, length us, event | category | flops | bytes accessed | tf_op | source)
XLA Modules:
  0.0 70.5 jit_solution(17098758130264441076)
XLA Ops:
  0.6 65.3 %shard_map.94 = (f32[512,1024]{1,0:T(8,128)}, f32[512,128]{1,0:T(8,128)}, f32[4,8,128]{2,1,0:T(8,128)}) custom-call(f32[4,1024,128]{2,1,0:T(8,128)} %bitcast.8, f32[3,256,256]{2,1,0:T(8,128)} %primal_ref.1, f32[3,256,256]{2,1,0:T(8,128)} %dual_ref.1, s32[3]{0:T(128)} %sizes_ref.1, s32[4,4,128]{2,1,0:T(4,128)} %bitcast.11, f32[4,128]{1,0:T(4,128)} %damp_ref.1, ...), custom_call_target="tpu_custom_call" | custom-call | tf_op jit(solution)/shard_map/pallas_call | solution.py:501
  66.0 0.0 copy-start
  66.0 0.0 copy-start.1
  66.0 3.2 %copy.14 = f32[4,128,1024]{2,1,0:T(8,128)} copy(f32[4,128,1024]{2,1,0:T(8,128)} %bitcast.9) | data formatting | bytes 4194304
  69.2 0.0 copy-done
  69.2 0.7 copy.15
  69.9 0.0 copy-done.1
  69.9 0.6 copy.16
Async XLA Ops:
  66.0 3.2 %copy-start = (f32[512,128]{1,0:T(8,128)S(1)}, f32[512,128]{1,0:T(8,128)}, u32[]{:S(2)}) copy-start(f32[512,128]{1,0:T(8,128)} %get-tuple-element.7) | copy-start | bytes 786436
  66.0 3.9 %copy-start.1 = (f32[4,8,128]{2,1,0:T(8,128)S(1)}, f32[4,8,128]{2,1,0:T(8,128)}, u32[]{:S(2)}) copy-start(f32[4,8,128]{2,1,0:T(8,128)} %get-tuple-element.14) | copy-start | bytes 49156
